TPU v7x, 32 devices: a whole 2x2x4 slice. The times are simulated.
32 devices in a mesh: expert: 8 (over y, x, core), tensor: 4 (over z).
Axes of the slice: x: 2, y: 2, z: 4, core: 2. Of those that a mesh axis runs over, the one named last changes fastest.
Arguments:
- flow_state: bfloat16 [8192, 2048], P('expert'), may hold values from -6 to 6
- norm_gain: float32 [2048], replicated, may hold values from 0.5 to 1.5
- expert_ids: int32 [8192, 6], P('expert'), may hold values from 0 to 15, all different within a row; in each aligned block of 1024 rows (0 to 1023, 1024 to 2047, ...) at most 512 rows name the same one
- gate_weights: float32 [8192, 6], P('expert'), may hold values from 0.1 to 1
- w_gate: bfloat16 [16, 704, 2048], P('expert', 'tensor'), may hold values from -0.125 to 0.125
- w_up: bfloat16 [16, 704, 2048], P('expert', 'tensor'), may hold values from -0.125 to 0.125
- w_down: bfloat16 [16, 704, 2048], P('expert', 'tensor'), may hold values from -0.21875 to 0.21875
Outputs:
- next_state: bfloat16 [8192, 2048], P('expert')
Inputs may be any that keep to these rules, and one draw needn't show every extreme that they name: `expert_ids`: each row names 6 different experts. Within the rows of one index of the expert axis no expert is named by more than 512 rows, a bound that some block reaches.
All inputs are finite; a program needn't handle non-finite values.
Results may differ from a plain program's by a relative error of at most 0.009.
Values may be sent and summed in bfloat16 or wider, within the bound.
A program may use at most 192 MiB of HBM per device.

v0:
```python
import jax
import jax.numpy as jnp
from jax import lax
from jax.sharding import PartitionSpec as P


def passed_along(shard, axis, by):
    count = lax.axis_size(axis)
    return lax.ppermute(shard, axis, [(i, (i + by) % count) for i in range(count)])


def shards(flow_state, norm_gain, expert_ids, gate_weights, w_gate, w_up, w_down):
    row_count = flow_state.shape[0]
    model_width = flow_state.shape[1]
    choose_count = expert_ids.shape[1]
    exp_local = w_gate.shape[0]
    groups = lax.axis_size("expert")
    my_index = lax.axis_index("expert")
    total_experts = exp_local * groups
    capacity = row_count // 2
    slot_total = row_count * choose_count
    state_wide = flow_state.astype(jnp.float32)
    mean_square = jnp.mean(state_wide * state_wide, axis=1, keepdims=True)
    normed = (state_wide * lax.rsqrt(mean_square + 1e-06) * norm_gain[None, :]).astype(jnp.bfloat16)
    flat_ids = expert_ids.reshape(-1)
    onehot = (flat_ids[:, None] == jnp.arange(total_experts, dtype=jnp.int32)[None, :]).astype(
        jnp.int32
    )
    running = jnp.cumsum(onehot, axis=0)
    slot_ids = jnp.sum(running * onehot, axis=1) - 1
    counts = jnp.sum(onehot, axis=0)
    offsets = jnp.cumsum(counts) - counts
    flat_place = jnp.sum(onehot * offsets[None, :], axis=1) + slot_ids
    flat_rows = jnp.arange(slot_total, dtype=jnp.int32) // choose_count
    place_rows = jnp.zeros((slot_total,), jnp.int32).at[flat_place].set(flat_rows)
    sorted_in = jnp.take(normed, place_rows, axis=0)

    def compute(
        out_buffer, group_start, group_count, begin, size, gate_block, up_block, down_block
    ):
        picked = lax.dynamic_slice_in_dim(sorted_in, begin, size, 0)
        gate_out = lax.dot_general(
            picked, gate_block, (((1,), (1,)), ((), ())), preferred_element_type=jnp.float32
        )
        up_out = lax.dot_general(
            picked, up_block, (((1,), (1,)), ((), ())), preferred_element_type=jnp.float32
        )
        activated = (jax.nn.silu(gate_out) * up_out).astype(jnp.bfloat16)
        output = jnp.dot(activated, down_block, preferred_element_type=jnp.float32).astype(
            jnp.bfloat16
        )
        position = begin + jnp.arange(size, dtype=jnp.int32)
        valid = (position >= group_start) & (position < group_start + group_count)
        previous = lax.dynamic_slice_in_dim(out_buffer, begin, size, 0)
        fresh = jnp.where(valid[:, None], output, previous)
        return lax.dynamic_update_slice_in_dim(out_buffer, fresh, begin, 0)

    def apply_block(out_buffer, blocks, source):
        gate_local, up_local, down_local = blocks
        for local_slot in range(exp_local):
            expert = source * exp_local + local_slot
            group_start = offsets[expert]
            group_count = counts[expert]
            window_start = jnp.minimum(group_start, slot_total - capacity)
            out_buffer = compute(
                out_buffer,
                group_start,
                group_count,
                window_start,
                capacity,
                gate_local[local_slot],
                up_local[local_slot],
                down_local[local_slot],
            )
        return out_buffer

    blocks = (w_gate, w_up, w_down)
    out_buffer = apply_block(jnp.zeros((slot_total, model_width), jnp.bfloat16), blocks, my_index)

    def rotate_turn(turn_index, carry):
        running_buffer, moving = carry
        moving = passed_along((moving[0], moving[1], moving[2]), "expert", 1)
        running_buffer = apply_block(running_buffer, moving, (my_index - turn_index - 1) % groups)
        return (running_buffer, moving)

    out_buffer, _ = lax.fori_loop(0, groups - 1, rotate_turn, (out_buffer, blocks))
    unsorted = jnp.take(out_buffer, flat_place, axis=0).reshape(
        row_count, choose_count, model_width
    )
    totals = jnp.zeros((row_count, model_width), jnp.float32)
    for choice_slot in range(choose_count):
        totals = (
            totals
            + unsorted[:, choice_slot, :].astype(jnp.float32)
            * gate_weights[:, choice_slot : choice_slot + 1]
        )
    summed = lax.psum(totals.astype(jnp.bfloat16), "tensor").astype(jnp.float32)
    return (state_wide + summed).astype(jnp.bfloat16)


def solution(mesh):
    return jax.shard_map(
        shards,
        mesh=mesh,
        in_specs=(
            P("expert", None),
            P(),
            P("expert", None),
            P("expert", None),
            P("expert", "tensor", None),
            P("expert", "tensor", None),
            P("expert", "tensor", None),
        ),
        out_specs=P("expert", None),
        check_vma=False,
    )
```

profile of v0, /device:TPU:0, one launch (start us, length us, event | category | flops | bytes accessed | tf_op | source)
XLA Modules:
  0.0 1125.9 jit_solution(10099816733646086782)
XLA Ops:
  19.6 23.0 %scatter_custom_fusion = s32[6144]{0:T(1024)S(1)} fusion(s32[6144]{0:T(1024)S(1)} %bitcast.130, s32[6144]{0:T(1024)S(1)} %add_select_fusion, s32[]{:T(128)} %constant.157.clone.1), kind=kCustom, calls=%fused_computation.131 | custom fusion | bytes 24580 | tf_op jit(solution)/shard_map/scatter | solution.py:35
  56.9 49.2 %gather_fusion = bf16[6144,2048]{1,0:T(8,128)(2,1)} fusion(bf16[1024,2048]{1,0:T(8,128)(2,1)} %fusion.36, s32[6144]{0:T(1024)S(1)} %fusion.104), kind=kCustom, calls=%fused_computation | custom fusion | bytes 50356224 | tf_op jit(solution)/shard_map/jit(_take)/gather | solution.py:36
  106.2 21.7 %broadcast_select_fusion = bf16[6144,2048]{1,0:T(8,128)(2,1)} fusion(bf16[6144,2048]{1,0:T(8,128)(2,1)} %gather_fusion, pred[6144]{0:T(1024)(128)(4,1)S(1)} %compare_and_fusion.1), kind=kLoop, calls=%fused_computation.40 | loop fusion | flops 12582912 | bytes 50337792 | tf_op jit(solution)/shard_map/jit(_take)/select_n | solution.py:36
  147.6 10.6 dynamic_update_slice.26
  173.0 624.1 %while.21 = (s32[]{:T(128)}, bf16[6144,2048]{1,0:T(8,128)(2,1)}, bf16[2,176,2048]{2,1,0:T(8,128)(2,1)}, bf16[2,176,2048]{2,1,0:T(8,128)(2,1)}, bf16[2,176,2048]{...) while((s32[]{:T(128)}, bf16[6144,2048]{1,0:T(8,128)(2,1)}, ...), condition=%wide.region_9.10_spmd, body=%wide.region_8.9_spmd.sunk | while | flops 2219872256 | bytes 74191640 | solution.py:86
  183.2 10.6 collective-permute-done.1
  197.1 12.3 %collective-permute-done = bf16[2,176,2048]{2,1,0:T(8,128)(2,1)S(1)} collective-permute-done((bf16[2,176,2048]{2,1,0:T(8,128)(2,1)}, bf16[2,176,2048]{2,1,0:T(8,128)(2,1)S(1)}, u32[]{:S(2)}, u32[]{:S(2)}) %collective-permute-start) | collective-permute-done | bytes 1441824 | tf_op jit(solution)/shard_map/while/body/eval_jaxpr/ppermute | solution.py:9
  209.3 15.6 %collective-permute-done.2 = bf16[2,176,2048]{2,1,0:T(8,128)(2,1)} collective-permute-done((bf16[2,176,2048]{2,1,0:T(8,128)(2,1)}, bf16[2,176,2048]{2,1,0:T(8,128)(2,1)}, u32[]{:S(2)}, u32[]{:S(2)}) %collective-permute-start.2) | collective-permute-done | bytes 1441824 | tf_op jit(solution)/shard_map/while/body/eval_jaxpr/ppermute | solution.py:9
  229.5 10.5 dynamic_update_slice.30
  271.5 11.0 collective-permute-done.1
  285.7 12.3 %collective-permute-done = bf16[2,176,2048]{2,1,0:T(8,128)(2,1)S(1)} collective-permute-done((bf16[2,176,2048]{2,1,0:T(8,128)(2,1)}, bf16[2,176,2048]{2,1,0:T(8,128)(2,1)S(1)}, u32[]{:S(2)}, u32[]{:S(2)}) %collective-permute-start) | collective-permute-done | bytes 1441824 | tf_op jit(solution)/shard_map/while/body/eval_jaxpr/ppermute | solution.py:9
  298.0 15.6 %collective-permute-done.2 = bf16[2,176,2048]{2,1,0:T(8,128)(2,1)} collective-permute-done((bf16[2,176,2048]{2,1,0:T(8,128)(2,1)}, bf16[2,176,2048]{2,1,0:T(8,128)(2,1)}, u32[]{:S(2)}, u32[]{:S(2)}) %collective-permute-start.2) | collective-permute-done | bytes 1441824 | tf_op jit(solution)/shard_map/while/body/eval_jaxpr/ppermute | solution.py:9
  359.8 11.9 %collective-permute-done.1 = bf16[2,176,2048]{2,1,0:T(8,128)(2,1)S(1)} collective-permute-done((bf16[2,176,2048]{2,1,0:T(8,128)(2,1)}, bf16[2,176,2048]{2,1,0:T(8,128)(2,1)S(1)}, u32[]{:S(2)}, u32[]{:S(2)}) %collective-permute-start.1) | collective-permute-done | bytes 1441824 | tf_op jit(solution)/shard_map/while/body/eval_jaxpr/ppermute | solution.py:9
  374.9 12.3 %collective-permute-done = bf16[2,176,2048]{2,1,0:T(8,128)(2,1)S(1)} collective-permute-done((bf16[2,176,2048]{2,1,0:T(8,128)(2,1)}, bf16[2,176,2048]{2,1,0:T(8,128)(2,1)S(1)}, u32[]{:S(2)}, u32[]{:S(2)}) %collective-permute-start) | collective-permute-done | bytes 1441824 | tf_op jit(solution)/shard_map/while/body/eval_jaxpr/ppermute | solution.py:9
  387.2 15.6 %collective-permute-done.2 = bf16[2,176,2048]{2,1,0:T(8,128)(2,1)} collective-permute-done((bf16[2,176,2048]{2,1,0:T(8,128)(2,1)}, bf16[2,176,2048]{2,1,0:T(8,128)(2,1)}, u32[]{:S(2)}, u32[]{:S(2)}) %collective-permute-start.2) | collective-permute-done | bytes 1441824 | tf_op jit(solution)/shard_map/while/body/eval_jaxpr/ppermute | solution.py:9
  448.9 12.0 %collective-permute-done.1 = bf16[2,176,2048]{2,1,0:T(8,128)(2,1)S(1)} collective-permute-done((bf16[2,176,2048]{2,1,0:T(8,128)(2,1)}, bf16[2,176,2048]{2,1,0:T(8,128)(2,1)S(1)}, u32[]{:S(2)}, u32[]{:S(2)}) %collective-permute-start.1) | collective-permute-done | bytes 1441824 | tf_op jit(solution)/shard_map/while/body/eval_jaxpr/ppermute | solution.py:9
  464.1 12.3 %collective-permute-done = bf16[2,176,2048]{2,1,0:T(8,128)(2,1)S(1)} collective-permute-done((bf16[2,176,2048]{2,1,0:T(8,128)(2,1)}, bf16[2,176,2048]{2,1,0:T(8,128)(2,1)S(1)}, u32[]{:S(2)}, u32[]{:S(2)}) %collective-permute-start) | collective-permute-done | bytes 1441824 | tf_op jit(solution)/shard_map/while/body/eval_jaxpr/ppermute | solution.py:9
  476.3 15.6 %collective-permute-done.2 = bf16[2,176,2048]{2,1,0:T(8,128)(2,1)} collective-permute-done((bf16[2,176,2048]{2,1,0:T(8,128)(2,1)}, bf16[2,176,2048]{2,1,0:T(8,128)(2,1)}, u32[]{:S(2)}, u32[]{:S(2)}) %collective-permute-start.2) | collective-permute-done | bytes 1441824 | tf_op jit(solution)/shard_map/while/body/eval_jaxpr/ppermute | solution.py:9
  537.6 12.4 %collective-permute-done.1 = bf16[2,176,2048]{2,1,0:T(8,128)(2,1)S(1)} collective-permute-done((bf16[2,176,2048]{2,1,0:T(8,128)(2,1)}, bf16[2,176,2048]{2,1,0:T(8,128)(2,1)S(1)}, u32[]{:S(2)}, u32[]{:S(2)}) %collective-permute-start.1) | collective-permute-done | bytes 1441824 | tf_op jit(solution)/shard_map/while/body/eval_jaxpr/ppermute | solution.py:9
  553.2 12.3 %collective-permute-done = bf16[2,176,2048]{2,1,0:T(8,128)(2,1)S(1)} collective-permute-done((bf16[2,176,2048]{2,1,0:T(8,128)(2,1)}, bf16[2,176,2048]{2,1,0:T(8,128)(2,1)S(1)}, u32[]{:S(2)}, u32[]{:S(2)}) %collective-permute-start) | collective-permute-done | bytes 1441824 | tf_op jit(solution)/shard_map/while/body/eval_jaxpr/ppermute | solution.py:9
  565.5 15.6 %collective-permute-done.2 = bf16[2,176,2048]{2,1,0:T(8,128)(2,1)} collective-permute-done((bf16[2,176,2048]{2,1,0:T(8,128)(2,1)}, bf16[2,176,2048]{2,1,0:T(8,128)(2,1)}, u32[]{:S(2)}, u32[]{:S(2)}) %collective-permute-start.2) | collective-permute-done | bytes 1441824 | tf_op jit(solution)/shard_map/while/body/eval_jaxpr/ppermute | solution.py:9
  627.3 11.9 %collective-permute-done.1 = bf16[2,176,2048]{2,1,0:T(8,128)(2,1)S(1)} collective-permute-done((bf16[2,176,2048]{2,1,0:T(8,128)(2,1)}, bf16[2,176,2048]{2,1,0:T(8,128)(2,1)S(1)}, u32[]{:S(2)}, u32[]{:S(2)}) %collective-permute-start.1) | collective-permute-done | bytes 1441824 | tf_op jit(solution)/shard_map/while/body/eval_jaxpr/ppermute | solution.py:9
  642.4 12.3 %collective-permute-done = bf16[2,176,2048]{2,1,0:T(8,128)(2,1)S(1)} collective-permute-done((bf16[2,176,2048]{2,1,0:T(8,128)(2,1)}, bf16[2,176,2048]{2,1,0:T(8,128)(2,1)S(1)}, u32[]{:S(2)}, u32[]{:S(2)}) %collective-permute-start) | collective-permute-done | bytes 1441824 | tf_op jit(solution)/shard_map/while/body/eval_jaxpr/ppermute | solution.py:9
  654.6 15.6 %collective-permute-done.2 = bf16[2,176,2048]{2,1,0:T(8,128)(2,1)} collective-permute-done((bf16[2,176,2048]{2,1,0:T(8,128)(2,1)}, bf16[2,176,2048]{2,1,0:T(8,128)(2,1)}, u32[]{:S(2)}, u32[]{:S(2)}) %collective-permute-start.2) | collective-permute-done | bytes 1441824 | tf_op jit(solution)/shard_map/while/body/eval_jaxpr/ppermute | solution.py:9
  715.4 13.0 %collective-permute-done.1 = bf16[2,176,2048]{2,1,0:T(8,128)(2,1)S(1)} collective-permute-done((bf16[2,176,2048]{2,1,0:T(8,128)(2,1)}, bf16[2,176,2048]{2,1,0:T(8,128)(2,1)S(1)}, u32[]{:S(2)}, u32[]{:S(2)}) %collective-permute-start.1) | collective-permute-done | bytes 1441824 | tf_op jit(solution)/shard_map/while/body/eval_jaxpr/ppermute | solution.py:9
  731.6 12.3 %collective-permute-done = bf16[2,176,2048]{2,1,0:T(8,128)(2,1)S(1)} collective-permute-done((bf16[2,176,2048]{2,1,0:T(8,128)(2,1)}, bf16[2,176,2048]{2,1,0:T(8,128)(2,1)S(1)}, u32[]{:S(2)}, u32[]{:S(2)}) %collective-permute-start) | collective-permute-done | bytes 1441824 | tf_op jit(solution)/shard_map/while/body/eval_jaxpr/ppermute | solution.py:9
  743.8 15.6 %collective-permute-done.2 = bf16[2,176,2048]{2,1,0:T(8,128)(2,1)} collective-permute-done((bf16[2,176,2048]{2,1,0:T(8,128)(2,1)}, bf16[2,176,2048]{2,1,0:T(8,128)(2,1)}, u32[]{:S(2)}, u32[]{:S(2)}) %collective-permute-start.2) | collective-permute-done | bytes 1441824 | tf_op jit(solution)/shard_map/while/body/eval_jaxpr/ppermute | solution.py:9
  797.1 57.9 %gather_fusion.1 = bf16[6144,2048]{1,0:T(8,128)(2,1)} fusion(bf16[6144,2048]{1,0:T(8,128)(2,1)} %get-tuple-element.228, s32[6144]{0:T(1024)} %broadcast_clamp_fusion), kind=kCustom, calls=%fused_computation.1 | custom fusion | bytes 50356224 | tf_op jit(solution)/shard_map/jit(_take)/gather | solution.py:87
  855.0 39.5 %gather.12 = bf16[1024,6,2048]{2,1,0:T(8,128)(2,1)} reshape(bf16[6144,2048]{1,0:T(8,128)(2,1)} %gather_fusion.1) | data formatting | bytes 50331648 | tf_op jit(solution)/shard_map/jit(_take)/gather | solution.py:87
  894.9 47.4 %copy_select_fusion = bf16[1024,6,2048]{2,0,1:T(8,128)(2,1)} fusion(bf16[1024,6,2048]{2,1,0:T(8,128)(2,1)} %gather.12, pred[1024,6]{0,1:T(8,128)(4,1)S(1)} %copy.12), kind=kLoop, calls=%fused_computation.39 | loop fusion | flops 12582912 | bytes 50337792 | tf_op jit(solution)/shard_map/jit(_take)/select_n | solution.py:87
  942.3 12.7 %fusion.39 = bf16[1024,2048]{1,0:T(8,128)(2,1)} fusion(bf16[1024,6,2048]{2,0,1:T(8,128)(2,1)} %copy_select_fusion, f32[1024]{0:T(1024)S(1)} %bitcast.137, f32[1024]{0:T(1024)S(1)} %bitcast.138, f32[1024]{0:T(1024)S(1)} %bitcast.134, f32[1024]{0:T(1024)S(1)} %bitcast.135, f32[1024]{0:T(1024)S(1)} %bitcast.136, f32[1024]{0:T(1024)S(1)} %bitcast.133), kind=kLoop, calls=%fused_computation.50 | loop fusion | flops 37748736 | bytes 29384704 | tf_op jit(solution)/shard_map/convert_element_type | solution.py:97
  955.0 156.3 %all-reduce.2.cloned.1.call-done = bf16[1024,2048]{1,0:T(8,128)(2,1)} async-done(((bf16[1024,2048]{1,0:T(8,128)(2,1)}), bf16[1024,2048]{1,0:T(8,128)(2,1)}) %all-reduce.2.cloned.1.call-update) | async-done | bytes 4194320 | tf_op jit(solution)/shard_map/psum | solution.py:97
  (202 shorter events, 373.8 us)
Async XLA Ops:
  6.5 1104.7 %all-reduce.2.cloned.1.call-start = ((), (), s32[]{:S(2)}) async-start(), calls=%async_computation | async-start | bytes 8388608 | tf_op jit(solution)/shard_map/psum | solution.py:97
  8.0 122.3 %copy-start.4 = (bf16[2,176,2048]{2,1,0:T(8,128)(2,1)}, bf16[2,176,2048]{2,1,0:T(8,128)(2,1)S(1)}, u32[]{:S(2)}) copy-start(bf16[2,176,2048]{2,1,0:T(8,128)(2,1)S(1)} %copy.40) | copy-start | bytes 4325380
  12.9 38.8 %copy-start.9 = (f32[2048]{0:T(1024)S(1)}, f32[2048]{0:T(1024)}, u32[]{:S(2)}) copy-start(f32[2048]{0:T(1024)} %param.10) | copy-start | bytes 24580
  174.1 19.7 %collective-permute-start.1 = (bf16[2,176,2048]{2,1,0:T(8,128)(2,1)}, bf16[2,176,2048]{2,1,0:T(8,128)(2,1)S(1)}, u32[]{:S(2)}, u32[]{:S(2)}) collective-permute-start(bf16[2,176,2048]{2,1,0:T(8,128)(2,1)} %get-tuple-element.352), channel_id=1, source_target_pairs={{0,4},{4,8},{8,12},{12,16},{16,20},{20,24},{24,28},{28,0},{1,5},{5... | collective-permute-start | bytes 4325384 | tf_op jit(solution)/shard_map/while/body/eval_jaxpr/ppermute | solution.py:9
  174.6 34.7 %collective-permute-start = (bf16[2,176,2048]{2,1,0:T(8,128)(2,1)}, bf16[2,176,2048]{2,1,0:T(8,128)(2,1)S(1)}, u32[]{:S(2)}, u32[]{:S(2)}) collective-permute-start(bf16[2,176,2048]{2,1,0:T(8,128)(2,1)} %copy-done.6), channel_id=1, source_target_pairs={{0,4},{4,8},{8,12},{12,16},{16,20},{20,24},{24,28},{28,0},{1,5},{5... | collective-permute-start | bytes 4325384 | tf_op jit(solution)/shard_map/while/body/eval_jaxpr/ppermute | solution.py:9
  177.3 47.6 %collective-permute-start.2 = (bf16[2,176,2048]{2,1,0:T(8,128)(2,1)}, bf16[2,176,2048]{2,1,0:T(8,128)(2,1)}, u32[]{:S(2)}, u32[]{:S(2)}) collective-permute-start(bf16[2,176,2048]{2,1,0:T(8,128)(2,1)} %get-tuple-element.351), channel_id=1, source_target_pairs={{0,4},{4,8},{8,12},{12,16},{16,20},{20,24},{24,28},{28,0},{1,5},{5... | collective-permute-start | bytes 4325384 | tf_op jit(solution)/shard_map/while/body/eval_jaxpr/ppermute | solution.py:9
  209.3 15.6 %copy-start = (bf16[2,176,2048]{2,1,0:T(8,128)(2,1)}, bf16[2,176,2048]{2,1,0:T(8,128)(2,1)S(1)}, u32[]{:S(2)}) copy-start(bf16[2,176,2048]{2,1,0:T(8,128)(2,1)S(1)} %collective-permute-done) | copy-start | bytes 4325380 | tf_op jit(solution)/shard_map/while
  263.0 19.5 %collective-permute-start.1 = (bf16[2,176,2048]{2,1,0:T(8,128)(2,1)}, bf16[2,176,2048]{2,1,0:T(8,128)(2,1)S(1)}, u32[]{:S(2)}, u32[]{:S(2)}) collective-permute-start(bf16[2,176,2048]{2,1,0:T(8,128)(2,1)} %get-tuple-element.352), channel_id=1, source_target_pairs={{0,4},{4,8},{8,12},{12,16},{16,20},{20,24},{24,28},{28,0},{1,5},{5... | collective-permute-start | bytes 4325384 | tf_op jit(solution)/shard_map/while/body/eval_jaxpr/ppermute | solution.py:9
  263.0 34.9 %collective-permute-start = (bf16[2,176,2048]{2,1,0:T(8,128)(2,1)}, bf16[2,176,2048]{2,1,0:T(8,128)(2,1)S(1)}, u32[]{:S(2)}, u32[]{:S(2)}) collective-permute-start(bf16[2,176,2048]{2,1,0:T(8,128)(2,1)} %copy-done.6), channel_id=1, source_target_pairs={{0,4},{4,8},{8,12},{12,16},{16,20},{20,24},{24,28},{28,0},{1,5},{5... | collective-permute-start | bytes 4325384 | tf_op jit(solution)/shard_map/while/body/eval_jaxpr/ppermute | solution.py:9
  265.6 48.0 %collective-permute-start.2 = (bf16[2,176,2048]{2,1,0:T(8,128)(2,1)}, bf16[2,176,2048]{2,1,0:T(8,128)(2,1)}, u32[]{:S(2)}, u32[]{:S(2)}) collective-permute-start(bf16[2,176,2048]{2,1,0:T(8,128)(2,1)} %get-tuple-element.351), channel_id=1, source_target_pairs={{0,4},{4,8},{8,12},{12,16},{16,20},{20,24},{24,28},{28,0},{1,5},{5... | collective-permute-start | bytes 4325384 | tf_op jit(solution)/shard_map/while/body/eval_jaxpr/ppermute | solution.py:9
  298.0 15.6 %copy-start = (bf16[2,176,2048]{2,1,0:T(8,128)(2,1)}, bf16[2,176,2048]{2,1,0:T(8,128)(2,1)S(1)}, u32[]{:S(2)}) copy-start(bf16[2,176,2048]{2,1,0:T(8,128)(2,1)S(1)} %collective-permute-done) | copy-start | bytes 4325380 | tf_op jit(solution)/shard_map/while
  352.2 19.5 %collective-permute-start.1 = (bf16[2,176,2048]{2,1,0:T(8,128)(2,1)}, bf16[2,176,2048]{2,1,0:T(8,128)(2,1)S(1)}, u32[]{:S(2)}, u32[]{:S(2)}) collective-permute-start(bf16[2,176,2048]{2,1,0:T(8,128)(2,1)} %get-tuple-element.352), channel_id=1, source_target_pairs={{0,4},{4,8},{8,12},{12,16},{16,20},{20,24},{24,28},{28,0},{1,5},{5... | collective-permute-start | bytes 4325384 | tf_op jit(solution)/shard_map/while/body/eval_jaxpr/ppermute | solution.py:9
  352.2 35.0 %collective-permute-start = (bf16[2,176,2048]{2,1,0:T(8,128)(2,1)}, bf16[2,176,2048]{2,1,0:T(8,128)(2,1)S(1)}, u32[]{:S(2)}, u32[]{:S(2)}) collective-permute-start(bf16[2,176,2048]{2,1,0:T(8,128)(2,1)} %copy-done.6), channel_id=1, source_target_pairs={{0,4},{4,8},{8,12},{12,16},{16,20},{20,24},{24,28},{28,0},{1,5},{5... | collective-permute-start | bytes 4325384 | tf_op jit(solution)/shard_map/while/body/eval_jaxpr/ppermute | solution.py:9
  353.8 48.9 %collective-permute-start.2 = (bf16[2,176,2048]{2,1,0:T(8,128)(2,1)}, bf16[2,176,2048]{2,1,0:T(8,128)(2,1)}, u32[]{:S(2)}, u32[]{:S(2)}) collective-permute-start(bf16[2,176,2048]{2,1,0:T(8,128)(2,1)} %get-tuple-element.351), channel_id=1, source_target_pairs={{0,4},{4,8},{8,12},{12,16},{16,20},{20,24},{24,28},{28,0},{1,5},{5... | collective-permute-start | bytes 4325384 | tf_op jit(solution)/shard_map/while/body/eval_jaxpr/ppermute | solution.py:9
  387.2 15.6 %copy-start = (bf16[2,176,2048]{2,1,0:T(8,128)(2,1)}, bf16[2,176,2048]{2,1,0:T(8,128)(2,1)S(1)}, u32[]{:S(2)}) copy-start(bf16[2,176,2048]{2,1,0:T(8,128)(2,1)S(1)} %collective-permute-done) | copy-start | bytes 4325380 | tf_op jit(solution)/shard_map/while
  441.3 19.5 %collective-permute-start.1 = (bf16[2,176,2048]{2,1,0:T(8,128)(2,1)}, bf16[2,176,2048]{2,1,0:T(8,128)(2,1)S(1)}, u32[]{:S(2)}, u32[]{:S(2)}) collective-permute-start(bf16[2,176,2048]{2,1,0:T(8,128)(2,1)} %get-tuple-element.352), channel_id=1, source_target_pairs={{0,4},{4,8},{8,12},{12,16},{16,20},{20,24},{24,28},{28,0},{1,5},{5... | collective-permute-start | bytes 4325384 | tf_op jit(solution)/shard_map/while/body/eval_jaxpr/ppermute | solution.py:9
  441.3 35.0 %collective-permute-start = (bf16[2,176,2048]{2,1,0:T(8,128)(2,1)}, bf16[2,176,2048]{2,1,0:T(8,128)(2,1)S(1)}, u32[]{:S(2)}, u32[]{:S(2)}) collective-permute-start(bf16[2,176,2048]{2,1,0:T(8,128)(2,1)} %copy-done.6), channel_id=1, source_target_pairs={{0,4},{4,8},{8,12},{12,16},{16,20},{20,24},{24,28},{28,0},{1,5},{5... | collective-permute-start | bytes 4325384 | tf_op jit(solution)/shard_map/while/body/eval_jaxpr/ppermute | solution.py:9
  441.6 50.3 %collective-permute-start.2 = (bf16[2,176,2048]{2,1,0:T(8,128)(2,1)}, bf16[2,176,2048]{2,1,0:T(8,128)(2,1)}, u32[]{:S(2)}, u32[]{:S(2)}) collective-permute-start(bf16[2,176,2048]{2,1,0:T(8,128)(2,1)} %get-tuple-element.351), channel_id=1, source_target_pairs={{0,4},{4,8},{8,12},{12,16},{16,20},{20,24},{24,28},{28,0},{1,5},{5... | collective-permute-start | bytes 4325384 | tf_op jit(solution)/shard_map/while/body/eval_jaxpr/ppermute | solution.py:9
  476.3 15.6 %copy-start = (bf16[2,176,2048]{2,1,0:T(8,128)(2,1)}, bf16[2,176,2048]{2,1,0:T(8,128)(2,1)S(1)}, u32[]{:S(2)}) copy-start(bf16[2,176,2048]{2,1,0:T(8,128)(2,1)S(1)} %collective-permute-done) | copy-start | bytes 4325380 | tf_op jit(solution)/shard_map/while
  530.5 19.5 %collective-permute-start.1 = (bf16[2,176,2048]{2,1,0:T(8,128)(2,1)}, bf16[2,176,2048]{2,1,0:T(8,128)(2,1)S(1)}, u32[]{:S(2)}, u32[]{:S(2)}) collective-permute-start(bf16[2,176,2048]{2,1,0:T(8,128)(2,1)} %get-tuple-element.352), channel_id=1, source_target_pairs={{0,4},{4,8},{8,12},{12,16},{16,20},{20,24},{24,28},{28,0},{1,5},{5... | collective-permute-start | bytes 4325384 | tf_op jit(solution)/shard_map/while/body/eval_jaxpr/ppermute | solution.py:9
  530.5 35.0 %collective-permute-start = (bf16[2,176,2048]{2,1,0:T(8,128)(2,1)}, bf16[2,176,2048]{2,1,0:T(8,128)(2,1)S(1)}, u32[]{:S(2)}, u32[]{:S(2)}) collective-permute-start(bf16[2,176,2048]{2,1,0:T(8,128)(2,1)} %copy-done.6), channel_id=1, source_target_pairs={{0,4},{4,8},{8,12},{12,16},{16,20},{20,24},{24,28},{28,0},{1,5},{5... | collective-permute-start | bytes 4325384 | tf_op jit(solution)/shard_map/while/body/eval_jaxpr/ppermute | solution.py:9
  530.5 50.5 %collective-permute-start.2 = (bf16[2,176,2048]{2,1,0:T(8,128)(2,1)}, bf16[2,176,2048]{2,1,0:T(8,128)(2,1)}, u32[]{:S(2)}, u32[]{:S(2)}) collective-permute-start(bf16[2,176,2048]{2,1,0:T(8,128)(2,1)} %get-tuple-element.351), channel_id=1, source_target_pairs={{0,4},{4,8},{8,12},{12,16},{16,20},{20,24},{24,28},{28,0},{1,5},{5... | collective-permute-start | bytes 4325384 | tf_op jit(solution)/shard_map/while/body/eval_jaxpr/ppermute | solution.py:9
  565.5 15.6 %copy-start = (bf16[2,176,2048]{2,1,0:T(8,128)(2,1)}, bf16[2,176,2048]{2,1,0:T(8,128)(2,1)S(1)}, u32[]{:S(2)}) copy-start(bf16[2,176,2048]{2,1,0:T(8,128)(2,1)S(1)} %collective-permute-done) | copy-start | bytes 4325380 | tf_op jit(solution)/shard_map/while
  619.6 19.5 %collective-permute-start.1 = (bf16[2,176,2048]{2,1,0:T(8,128)(2,1)}, bf16[2,176,2048]{2,1,0:T(8,128)(2,1)S(1)}, u32[]{:S(2)}, u32[]{:S(2)}) collective-permute-start(bf16[2,176,2048]{2,1,0:T(8,128)(2,1)} %get-tuple-element.352), channel_id=1, source_target_pairs={{0,4},{4,8},{8,12},{12,16},{16,20},{20,24},{24,28},{28,0},{1,5},{5... | collective-permute-start | bytes 4325384 | tf_op jit(solution)/shard_map/while/body/eval_jaxpr/ppermute | solution.py:9
  619.6 35.0 %collective-permute-start = (bf16[2,176,2048]{2,1,0:T(8,128)(2,1)}, bf16[2,176,2048]{2,1,0:T(8,128)(2,1)S(1)}, u32[]{:S(2)}, u32[]{:S(2)}) collective-permute-start(bf16[2,176,2048]{2,1,0:T(8,128)(2,1)} %copy-done.6), channel_id=1, source_target_pairs={{0,4},{4,8},{8,12},{12,16},{16,20},{20,24},{24,28},{28,0},{1,5},{5... | collective-permute-start | bytes 4325384 | tf_op jit(solution)/shard_map/while/body/eval_jaxpr/ppermute | solution.py:9
  619.6 50.5 %collective-permute-start.2 = (bf16[2,176,2048]{2,1,0:T(8,128)(2,1)}, bf16[2,176,2048]{2,1,0:T(8,128)(2,1)}, u32[]{:S(2)}, u32[]{:S(2)}) collective-permute-start(bf16[2,176,2048]{2,1,0:T(8,128)(2,1)} %get-tuple-element.351), channel_id=1, source_target_pairs={{0,4},{4,8},{8,12},{12,16},{16,20},{20,24},{24,28},{28,0},{1,5},{5... | collective-permute-start | bytes 4325384 | tf_op jit(solution)/shard_map/while/body/eval_jaxpr/ppermute | solution.py:9
  708.8 19.5 %collective-permute-start.1 = (bf16[2,176,2048]{2,1,0:T(8,128)(2,1)}, bf16[2,176,2048]{2,1,0:T(8,128)(2,1)S(1)}, u32[]{:S(2)}, u32[]{:S(2)}) collective-permute-start(bf16[2,176,2048]{2,1,0:T(8,128)(2,1)} %get-tuple-element.352), channel_id=1, source_target_pairs={{0,4},{4,8},{8,12},{12,16},{16,20},{20,24},{24,28},{28,0},{1,5},{5... | collective-permute-start | bytes 4325384 | tf_op jit(solution)/shard_map/while/body/eval_jaxpr/ppermute | solution.py:9
  708.8 35.0 %collective-permute-start = (bf16[2,176,2048]{2,1,0:T(8,128)(2,1)}, bf16[2,176,2048]{2,1,0:T(8,128)(2,1)S(1)}, u32[]{:S(2)}, u32[]{:S(2)}) collective-permute-start(bf16[2,176,2048]{2,1,0:T(8,128)(2,1)} %copy-done.6), channel_id=1, source_target_pairs={{0,4},{4,8},{8,12},{12,16},{16,20},{20,24},{24,28},{28,0},{1,5},{5... | collective-permute-start | bytes 4325384 | tf_op jit(solution)/shard_map/while/body/eval_jaxpr/ppermute | solution.py:9
  708.8 50.5 %collective-permute-start.2 = (bf16[2,176,2048]{2,1,0:T(8,128)(2,1)}, bf16[2,176,2048]{2,1,0:T(8,128)(2,1)}, u32[]{:S(2)}, u32[]{:S(2)}) collective-permute-start(bf16[2,176,2048]{2,1,0:T(8,128)(2,1)} %get-tuple-element.351), channel_id=1, source_target_pairs={{0,4},{4,8},{8,12},{12,16},{16,20},{20,24},{24,28},{28,0},{1,5},{5... | collective-permute-start | bytes 4325384 | tf_op jit(solution)/shard_map/while/body/eval_jaxpr/ppermute | solution.py:9
  743.8 15.6 %copy-start = (bf16[2,176,2048]{2,1,0:T(8,128)(2,1)}, bf16[2,176,2048]{2,1,0:T(8,128)(2,1)S(1)}, u32[]{:S(2)}) copy-start(bf16[2,176,2048]{2,1,0:T(8,128)(2,1)S(1)} %collective-permute-done) | copy-start | bytes 4325380 | tf_op jit(solution)/shard_map/while
  854.9 39.5 %copy-start.2 = (s32[1024,6]{1,0:T(8,128)S(1)}, s32[1024,6]{1,0:T(8,128)}, u32[]{:S(2)}) copy-start(s32[1024,6]{1,0:T(8,128)} %add.329) | copy-start | bytes 73732
  854.9 39.9 %copy-start.8 = (f32[1024,6]{0,1:T(8,128)S(1)}, f32[1024,6]{0,1:T(8,128)}, u32[]{:S(2)}) copy-start(f32[1024,6]{0,1:T(8,128)} %param.12) | copy-start | bytes 73732
  (18 other events, 71.4 us)
Sparse Core Ops, SparseCore 0:
  955.1 156.1 all-reduce.1
where the time goes:
time: 1130 us
  waiting for transfers between devices  434 us (38%)
  local copies, waits for them, and re-layouts  396 us (35%)
  matrix products  123 us (11%)
  other arithmetic  115 us (10%)
  loops' own time  28.3 us (3%)
  between operations  17.5 us (2%)
  starting transfers between devices  12.6 us (1%)
    ppermute x21, waiting for transfers between devices, passed_along(): lax.ppermute(shard, axis, [(i, (i + by) % count) for i in range(count)])  277 us
    dynamic_update_slice x16, local copies, waits for them, and re-layouts, compute(): return lax.dynamic_update_slice_in_dim(out_buffer, fresh, begin, 0)  168 us
    psum x1, waiting for transfers between devices, shards(): summed = lax.psum(totals.astype(jnp.bfloat16), 'tensor').astype(jnp.float32)  156 us
    gather x2, local copies, waits for them, and re-layouts, shards(): jnp.take(out_buffer, flat_place, axis=0)  97.4 us
    dot_general x16, matrix products, compute(): jnp.dot(activated, down_block, preferred_element_type=jnp.float32)  72.7 us
    gather x1, local copies, waits for them, and re-layouts, shards(): sorted_in = jnp.take(normed, place_rows, axis=0)  49.2 us
    select_n x2, other arithmetic, shards(): jnp.take(out_buffer, flat_place, axis=0)  47.4 us
    dot_general x14, matrix products, compute(): lax.dot_general(picked, up_block, (((1,), (1,)), ((), ())), preferred_ele...  44.7 us
  transfers between devices with their start and end apart: 22, of which 22 were waited for; matrix products, arithmetic and copies ran while one was open for 3% of the time, Pallas kernels for 0%

commit v1 on v0

v1 whole, which is shorter than its diff:
```python
import functools

import jax
import jax.numpy as jnp
from jax import lax
from jax.experimental import pallas as pl
from jax.experimental.pallas import tpu as pltpu
from jax.sharding import PartitionSpec as P

MESH = pl.DeviceIdType.MESH
CHUNKS = 4
ROW_TILE = 256


def kernel(
    groups,
    state_hbm,
    gain_ref,
    ids_ref,
    gw_ref,
    wg_hbm,
    wu_hbm,
    wd_hbm,
    out_hbm,
    gbuf,
    ubuf,
    dbuf,
    part,
    nrm,
    act,
    recv_sem,
    send_sem,
    local_sem,
    state_sem,
    out_sem,
):
    rows, width = nrm.shape
    exp_local, hidden, _ = wg_hbm.shape
    experts = gbuf.shape[0]
    ny = groups // 4
    half = width // 2
    col = width // CHUNKS
    me = lax.axis_index("expert")
    my_c = lax.rem(me, 2)
    my_x = lax.rem(me // 2, 2)
    my_y = me // 4

    def device(j, flip_x, flip_c):
        y = lax.rem(my_y + j, ny)
        x = 1 - my_x if flip_x else my_x
        c = 1 - my_c if flip_c else my_c
        return (y * 2 + x) * 2 + c

    x_peer = device(0, True, False)
    y_peers = [device(j, False, False) for j in range(1, ny)]
    sibling = device(0, False, True)

    pieces = []
    items = []
    for l in range(exp_local):
        p_half, q_half = [], []
        for src, buf in ((wg_hbm, gbuf), (wu_hbm, ubuf)):
            p_half.append(len(pieces))
            pieces.append((l, src, buf, 0, half))
            q_half.append(len(pieces))
            pieces.append((l, src, buf, half, half))
        items.append((p_half, q_half))
    for k in range(CHUNKS):
        p_half, q_half = [], []
        for l in range(exp_local):
            (p_half if l % 2 == 0 else q_half).append(len(pieces))
            pieces.append((l, wd_hbm, dbuf, k * col, col))
        items.append((p_half, q_half))

    def held(piece, source):
        l, _, buf, start, size = pieces[piece]
        return buf.at[source * exp_local + l, :, pl.ds(start, size)]

    def own(piece):
        l, src, _, start, size = pieces[piece]
        return src.at[l, :, pl.ds(start, size)]

    sent = []

    def send(piece, source, target, kind, is_own=False):
        copy = pltpu.make_async_remote_copy(
            src_ref=own(piece) if is_own else held(piece, source),
            dst_ref=held(piece, source),
            send_sem=send_sem.at[kind, piece, source],
            recv_sem=recv_sem.at[piece, source],
            device_id={"expert": target},
            device_id_type=MESH,
        )
        copy.start()
        sent.append(copy)

    def arrived(piece, source):
        pltpu.make_async_remote_copy(
            src_ref=held(piece, source),
            dst_ref=held(piece, source),
            send_sem=send_sem.at[0, piece, source],
            recv_sem=recv_sem.at[piece, source],
            device_id={"expert": sibling},
            device_id_type=MESH,
        ).wait_recv()

    def to_x(piece, source, is_own=False):
        send(piece, source, x_peer, 0, is_own)

    def to_core(piece, source, is_own=False):
        send(piece, source, sibling, 1, is_own)

    def to_y(piece, source, is_own=False):
        for n, peer in enumerate(y_peers):
            send(piece, source, peer, 2 + n, is_own)

    def start_own(item):
        p_half, q_half = items[item]
        for p, q in zip(p_half, q_half):
            to_x(p, me, True)
            to_y(q, me, True)
        for p, q in zip(p_half, q_half):
            to_x(q, me, True)
            to_y(p, me, True)
        for p, q in zip(p_half, q_half):
            to_core(p, me, True)
            to_core(q, me, True)

    def forward(item):
        p_half, q_half = items[item]
        for p, q in zip(p_half, q_half):
            arrived(p, x_peer)
            to_y(p, x_peer)
            to_core(p, x_peer)
            for peer in y_peers:
                arrived(q, peer)
                to_x(q, peer)
                to_core(q, peer)

    def second(item):
        p_half, q_half = items[item]
        for p, q in zip(p_half, q_half):
            arrived(q, x_peer)
            to_core(q, x_peer)
            for peer in y_peers:
                arrived(p, peer)
                to_core(p, peer)

    corners = [device(j, True, False) for j in range(1, ny)]

    def third(item):
        p_half, q_half = items[item]
        for p, q in zip(p_half, q_half):
            for corner in corners:
                arrived(p, corner)
                to_core(p, corner)
                arrived(q, corner)
                to_core(q, corner)

    def from_core(item, sources):
        p_half, q_half = items[item]
        for source in sources:
            for piece in p_half + q_half:
                arrived(piece, source)

    sib_x = device(0, True, True)
    sib_y = [device(j, False, True) for j in range(1, ny)]
    sib_corners = [device(j, True, True) for j in range(1, ny)]

    barrier = pltpu.get_barrier_semaphore()
    peers = [x_peer, sibling] + y_peers
    for peer in peers:
        pl.semaphore_signal(barrier, inc=1, device_id={"expert": peer}, device_id_type=MESH)
    pl.semaphore_wait(barrier, len(peers))

    start_own(0)
    load_state = pltpu.make_async_copy(state_hbm, part, state_sem)
    load_state.start()
    loads = []
    for n, (src, buf) in enumerate(((wg_hbm, gbuf), (wu_hbm, ubuf), (wd_hbm, dbuf))):
        copy = pltpu.make_async_copy(src, buf.at[pl.ds(me * exp_local, exp_local)], local_sem.at[n])
        copy.start()
        loads.append(copy)
    load_state.wait()

    @pl.loop(0, rows // 64)
    def _(i):
        span = pl.ds(pl.multiple_of(i * 64, 64), 64)
        wide = part[span, :].astype(jnp.float32)
        mean_square = jnp.mean(wide * wide, axis=1, keepdims=True)
        nrm[span, :] = (wide * lax.rsqrt(mean_square + 1e-06) * gain_ref[...]).astype(jnp.bfloat16)

    for copy in loads:
        copy.wait()

    def hidden_units(source, l):
        expert = source * exp_local + l

        @pl.loop(0, rows // ROW_TILE)
        def _(i):
            span = pl.ds(pl.multiple_of(i * ROW_TILE, ROW_TILE), ROW_TILE)
            a = nrm[span, :]
            dims = (((1,), (1,)), ((), ()))
            g = lax.dot_general(a, gbuf[expert], dims, preferred_element_type=jnp.float32)
            u = lax.dot_general(a, ubuf[expert], dims, preferred_element_type=jnp.float32)
            scale = jnp.sum(
                jnp.where(ids_ref[span, :] == expert, gw_ref[span, :], 0.0), axis=1, keepdims=True
            )
            act[expert, span, :] = (g / (1.0 + jnp.exp(-g)) * u * scale).astype(jnp.bfloat16)

    outs = []

    def outputs(k):
        @pl.loop(0, rows // ROW_TILE)
        def _(i):
            span = pl.ds(pl.multiple_of(i * ROW_TILE, ROW_TILE), ROW_TILE)
            total = jnp.zeros((ROW_TILE, col), jnp.float32)
            for expert in range(experts):
                total = total + jnp.dot(
                    act[expert, span, :],
                    dbuf[expert, :, k * col : (k + 1) * col],
                    preferred_element_type=jnp.float32,
                )
            part[span, k * col : (k + 1) * col] = total.astype(jnp.bfloat16)

        cols = pl.ds(k * col, col)
        copy = pltpu.make_async_copy(part.at[:, cols], out_hbm.at[:, cols], out_sem.at[k])
        copy.start()
        outs.append(copy)

    last = len(items) - 1
    for item in range(len(items)):
        forward(item)
        if item < last:
            start_own(item + 1)
        if item < exp_local:
            hidden_units(me, item)
            from_core(item, [sibling])
            hidden_units(sibling, item)
            second(item)
            for source in [x_peer] + y_peers:
                hidden_units(source, item)
            for source in [sib_x] + sib_y:
                from_core(item, [source])
                hidden_units(source, item)
            third(item)
            for source in corners:
                hidden_units(source, item)
            for source in sib_corners:
                from_core(item, [source])
                hidden_units(source, item)
        else:
            second(item)
            third(item)
            from_core(item, [sibling, sib_x] + sib_y + sib_corners)
            outputs(item - exp_local)
    for copy in sent:
        copy.wait_send()
    for copy in outs:
        copy.wait()


def shards(flow_state, norm_gain, expert_ids, gate_weights, w_gate, w_up, w_down):
    rows, width = flow_state.shape
    exp_local, hidden, _ = w_gate.shape
    groups = lax.axis_size("expert")
    experts = exp_local * groups
    n_pieces = exp_local * (4 + CHUNKS)
    weights = pltpu.VMEM((experts, hidden, width), jnp.bfloat16)
    any_space = pl.BlockSpec(memory_space=pl.ANY)
    vmem = pl.BlockSpec(memory_space=pltpu.VMEM)
    partial = pl.pallas_call(
        functools.partial(kernel, groups),
        out_shape=jax.ShapeDtypeStruct((rows, width), jnp.bfloat16),
        in_specs=[any_space, vmem, vmem, vmem, any_space, any_space, any_space],
        out_specs=any_space,
        scratch_shapes=[
            weights,
            weights,
            weights,
            pltpu.VMEM((rows, width), jnp.bfloat16),
            pltpu.VMEM((rows, width), jnp.bfloat16),
            pltpu.VMEM((experts, rows, hidden), jnp.bfloat16),
            pltpu.SemaphoreType.DMA((n_pieces, groups)),
            pltpu.SemaphoreType.DMA((groups // 4 + 1, n_pieces, groups)),
            pltpu.SemaphoreType.DMA((3,)),
            pltpu.SemaphoreType.DMA,
            pltpu.SemaphoreType.DMA((CHUNKS,)),
        ],
        compiler_params=pltpu.CompilerParams(
            collective_id=0, has_side_effects=True, vmem_limit_bytes=66 * 1000 * 1000
        ),
    )(
        flow_state,
        norm_gain.reshape(1, width),
        expert_ids,
        gate_weights,
        w_gate,
        w_up,
        w_down,
    )
    summed = lax.psum(partial, "tensor").astype(jnp.float32)
    return (flow_state.astype(jnp.float32) + summed).astype(jnp.bfloat16)


def solution(mesh):
    return jax.shard_map(
        shards,
        mesh=mesh,
        in_specs=(
            P("expert", None),
            P(),
            P("expert", None),
            P("expert", None),
            P("expert", "tensor", None),
            P("expert", "tensor", None),
            P("expert", "tensor", None),
        ),
        out_specs=P("expert", None),
        check_vma=False,
    )
```

time: 1130 us -> 341 us (0.30)
  local copies, waits for them, and re-layouts: 396 us -> 3.55 us
  waiting for transfers between devices: 434 us -> 155 us
  Pallas kernels: 0 us -> 160 us
  matrix products: 123 us -> 0 us
  other arithmetic: 115 us -> 7.77 us
  loops' own time: 28.3 us -> 0 us
  starting transfers between devices: 12.6 us -> 0.01 us
    ppermute x21 -> x0, waiting for transfers between devices: 277 us -> none  [passed_along(): lax.ppermute(shard, axis, [(i, (i + by) % count) for i in range(count)])]
    dynamic_update_slice x16 -> x0, local copies, waits for them, and re-layouts: 168 us -> none  [compute(): return lax.dynamic_update_slice_in_dim(out_buffer, fresh, begin, 0)]
    pallas_call x0 -> x1, Pallas kernels: none -> 160 us  [shards(): pl.pallas_call(functools.partial(kernel, groups), out_shape=jax.ShapeDtyp...]
    gather x3 -> x0, local copies, waits for them, and re-layouts: 147 us -> none  [the longest x2 97.4 us: shards(): jnp.take(out_buffer, flat_place, axis=0)]
    dot_general x32 -> x0, matrix products: 123 us -> none  [the longest x16 72.7 us: compute(): jnp.dot(activated, down_block, preferred_element_type=jnp.float32)]
    select_n x4 -> x0, other arithmetic: 69.2 us -> none  [the longest x2 47.4 us: shards(): jnp.take(out_buffer, flat_place, axis=0)]
    while x63 -> x0, local copies, waits for them, and re-layouts: 35.8 us -> none
    another operation x1 -> x0, loops' own time: 28.3 us -> none  [shards(): lax.fori_loop(0, groups - 1, rotate_turn, (out_buffer, blocks))]
  transfers between devices with their start and end apart: 22 -> 1, of which waited for: 22 -> 1; matrix products, arithmetic and copies ran while one was open for 3% -> 0% of each run, Pallas kernels for 0% -> 0%
where the time goes in v1:
time: 341 us
  Pallas kernels  160 us (47%)
  waiting for transfers between devices  155 us (45%)
  between operations  13.4 us (4%)
  other arithmetic  7.77 us (2%)
  local copies, waits for them, and re-layouts  3.55 us (1%)
    pallas_call x1, Pallas kernels, shards(): pl.pallas_call(functools.partial(kernel, groups), out_shape=jax.ShapeDtyp...  160 us
    psum x1, waiting for transfers between devices, shards(): summed = lax.psum(partial, 'tensor').astype(jnp.float32)  155 us
    convert_element_type x1, other arithmetic, shards(): return (flow_state.astype(jnp.float32) + summed).astype(jnp.bfloat16)  7.77 us
  transfers between devices with their start and end apart: 1, of which 1 were waited for; matrix products, arithmetic and copies ran while one was open for 0% of the time, Pallas kernels for 0%

profile of v1, /device:TPU:0, one launch (start us, length us, event | category | flops | bytes accessed | tf_op | source)
XLA Modules:
  0.0 340.6 jit_solution(7252997380653576733)
XLA Ops:
  6.5 0.0 all-reduce.2.cloned.1.call-start
  6.5 1.8 copy.8.ids_ref
  8.3 1.8 copy.9.gw_ref
  10.1 160.5 %shard_map.73 = bf16[1024,2048]{1,0:T(8,128)(2,1)} custom-call(bf16[1024,2048]{1,0:T(8,128)(2,1)} %state_hbm.1, f32[1,2048]{1,0:T(1,128)} %bitcast.1, s32[1024,6]{1,0:T(8,128)} %copy.8.ids_ref, f32[1024,6]{1,0:T(8,128)} %copy.9.gw_ref, bf16[2,176,2048]{2,1,0:T(8,128)(2,1)} %wg_hbm.1, bf16[2,176,2048]{2,1,0:T(8,128)(2,1)} %wu_hbm.1, bf16[2,176,2048]{2,1,0:T(8,128)(2,1)} %wd_hbm.1), custom_call_target="tpu_custom_call" | custom-call | tf_op jit(solution)/shard_map/pallas_call | solution.py:272
  170.6 0.0 all-reduce.2.cloned.1.call-update
  170.6 155.3 %all-reduce.2.cloned.1.call-done = bf16[1024,2048]{1,0:T(8,128)(2,1)} async-done(((bf16[1024,2048]{1,0:T(8,128)(2,1)}), bf16[1024,2048]{1,0:T(8,128)(2,1)}) %all-reduce.2.cloned.1.call-update) | async-done | bytes 4194320 | tf_op jit(solution)/shard_map/psum | solution.py:302
  325.9 7.8 %add_convert_fusion = bf16[1024,2048]{1,0:T(8,128)(2,1)} fusion(bf16[1024,2048]{1,0:T(8,128)(2,1)} %all-reduce.2.cloned.1.call-done, bf16[1024,2048]{1,0:T(8,128)(2,1)} %state_hbm.1), kind=kLoop, calls=%fused_computation | loop fusion | flops 8388608 | bytes 12582912 | tf_op jit(solution)/shard_map/convert_element_type | solution.py:303
Async XLA Ops:
  6.5 319.4 %all-reduce.2.cloned.1.call-start = ((), (), s32[]{:S(2)}) async-start(), calls=%async_computation | async-start | bytes 8388608 | tf_op jit(solution)/shard_map/psum | solution.py:302
Sparse Core Ops, SparseCore 0:
  170.7 155.1 all-reduce.1

commit v2 on v1

--- a/solution.py
+++ b/solution.py
@@ -14,6 +14,7 @@
 
 def kernel(
     groups,
+    slices,
     state_hbm,
     gain_ref,
     ids_ref,
@@ -28,11 +29,18 @@
     part,
     nrm,
     act,
+    zin,
+    own_state,
     recv_sem,
     send_sem,
     local_sem,
     state_sem,
     out_sem,
+    rs_recv,
+    rs_send,
+    fin_send,
+    ag_recv,
+    ag_send,
 ):
     rows, width = nrm.shape
     exp_local, hidden, _ = wg_hbm.shape
@@ -40,6 +48,8 @@
     ny = groups // 4
     half = width // 2
     col = width // CHUNKS
+    z_rows = rows // slices
+    z_tile = min(z_rows, 64)
     me = lax.axis_index("expert")
     my_c = lax.rem(me, 2)
     my_x = lax.rem(me // 2, 2)
@@ -167,10 +177,13 @@
     sib_y = [device(j, False, True) for j in range(1, ny)]
     sib_corners = [device(j, True, True) for j in range(1, ny)]
 
+    at = lax.axis_index("tensor")
+    right, left = lax.rem(at + 1, slices), lax.rem(at + slices - 1, slices)
     barrier = pltpu.get_barrier_semaphore()
-    peers = [x_peer, sibling] + y_peers
+    peers = [{"expert": peer} for peer in [x_peer, sibling] + y_peers]
+    peers += [{"tensor": right}, {"tensor": left}]
     for peer in peers:
-        pl.semaphore_signal(barrier, inc=1, device_id={"expert": peer}, device_id_type=MESH)
+        pl.semaphore_signal(barrier, inc=1, device_id=peer, device_id_type=MESH)
     pl.semaphore_wait(barrier, len(peers))
 
     start_own(0)
@@ -181,6 +194,11 @@
         copy = pltpu.make_async_copy(src, buf.at[pl.ds(me * exp_local, exp_local)], local_sem.at[n])
         copy.start()
         loads.append(copy)
+    load_own = pltpu.make_async_copy(
+        state_hbm.at[pl.ds(at * z_rows, z_rows)], own_state, local_sem.at[3]
+    )
+    load_own.start()
+    loads.append(load_own)
     load_state.wait()
 
     @pl.loop(0, rows // 64)
@@ -207,8 +225,6 @@
                 jnp.where(ids_ref[span, :] == expert, gw_ref[span, :], 0.0), axis=1, keepdims=True
             )
             act[expert, span, :] = (g / (1.0 + jnp.exp(-g)) * u * scale).astype(jnp.bfloat16)
-
-    outs = []
 
     def outputs(k):
         @pl.loop(0, rows // ROW_TILE)
@@ -223,13 +239,170 @@
                 )
             part[span, k * col : (k + 1) * col] = total.astype(jnp.bfloat16)
 
-        cols = pl.ds(k * col, col)
-        copy = pltpu.make_async_copy(part.at[:, cols], out_hbm.at[:, cols], out_sem.at[k])
-        copy.start()
-        outs.append(copy)
+    def block(ref, k, q):
+        return ref.at[pl.ds(pl.multiple_of(q * z_rows, z_rows), z_rows), pl.ds(k * col, col)]
+
+    def sum_copy(k, q, slot, target):
+        return pltpu.make_async_remote_copy(
+            src_ref=block(part, k, q),
+            dst_ref=zin.at[k, slot],
+            send_sem=rs_send.at[k, q],
+            recv_sem=rs_recv.at[k, slot],
+            device_id={"tensor": target},
+            device_id_type=MESH,
+        )
+
+    def final_copy(k, q, source, sem, target):
+        return pltpu.make_async_remote_copy(
+            src_ref=block(source, k, q),
+            dst_ref=block(out_hbm, k, q),
+            send_sem=sem,
+            recv_sem=ag_recv.at[k, q],
+            device_id={"tensor": target},
+            device_id_type=MESH,
+        )
+
+    def local_copy(k):
+        return pltpu.make_async_copy(block(part, k, at), block(out_hbm, k, at), out_sem.at[k])
+
+    def add_in(k, q, slot):
+        sum_copy(k, q, slot, right).wait_recv()
+
+        @pl.loop(0, z_rows // z_tile)
+        def _(i):
+            inner = pl.ds(pl.multiple_of(i * z_tile, z_tile), z_tile)
+            span = pl.ds(pl.multiple_of(q * z_rows + i * z_tile, z_tile), z_tile)
+            total = part[span, k * col : (k + 1) * col].astype(jnp.float32)
+            total = total + zin[k, slot, inner, :].astype(jnp.float32)
+            part[span, k * col : (k + 1) * col] = total.astype(jnp.bfloat16)
+
+    def sums(k, d):
+        @pl.when(at + d < slices)
+        def _():
+            @pl.when(at > 0)
+            def _():
+                add_in(k, at + d, at + d)
+
+            sum_copy(k, at + d, at + d, right).start()
+
+        @pl.when(at - d >= 0)
+        def _():
+            @pl.when(at < slices - 1)
+            def _():
+                add_in(k, at - d, at - d)
+
+            sum_copy(k, at - d, slices if d == 1 else at - d, left).start()
+
+    def finish(k):
+        cols = slice(k * col, (k + 1) * col)
+
+        def rounds(slots):
+            for slot in slots:
+                sum_copy(k, at, slot, right).wait_recv()
+
+            @pl.loop(0, z_rows // z_tile)
+            def _(i):
+                inner = pl.ds(pl.multiple_of(i * z_tile, z_tile), z_tile)
+                span = pl.ds(pl.multiple_of(at * z_rows + i * z_tile, z_tile), z_tile)
+                total = part[span, cols].astype(jnp.float32)
+                for slot in slots:
+                    total = total + zin[k, slot, inner, :].astype(jnp.float32)
+                total = total + own_state[inner, cols].astype(jnp.float32)
+                part[span, cols] = total.astype(jnp.bfloat16)
+
+        @pl.when(at == 0)
+        def _():
+            rounds([slices])
+
+        @pl.when(at == slices - 1)
+        def _():
+            rounds([at])
+
+        @pl.when((at > 0) & (at < slices - 1))
+        def _():
+            rounds([at, slices])
+
+        @pl.when(at < slices - 1)
+        def _():
+            final_copy(k, at, part, fin_send.at[k, 0], right).start()
+
+        @pl.when(at > 0)
+        def _():
+            final_copy(k, at, part, fin_send.at[k, 1], left).start()
+
+        local_copy(k).start()
+
+    def passes(k, d):
+        @pl.when(at - d >= 0)
+        def _():
+            final_copy(k, at - d, out_hbm, ag_send.at[k, at - d], right).wait_recv()
+
+            @pl.when(at < slices - 1)
+            def _():
+                final_copy(k, at - d, out_hbm, ag_send.at[k, at - d], right).start()
+
+        @pl.when(at + d < slices)
+        def _():
+            final_copy(k, at + d, out_hbm, ag_send.at[k, at + d], left).wait_recv()
+
+            @pl.when(at > 0)
+            def _():
+                final_copy(k, at + d, out_hbm, ag_send.at[k, at + d], left).start()
+
+    def drain(k):
+        for d in range(1, slices):
+
+            @pl.when(at + d < slices)
+            def _():
+                sum_copy(k, at + d, at + d, right).wait_send()
+
+                @pl.when(at > 0)
+                def _():
+                    final_copy(k, at + d, out_hbm, ag_send.at[k, at + d], left).wait_send()
+
+            @pl.when(at - d >= 0)
+            def _():
+                sum_copy(k, at - d, at - d, left).wait_send()
+
+                @pl.when(at < slices - 1)
+                def _():
+                    final_copy(k, at - d, out_hbm, ag_send.at[k, at - d], right).wait_send()
+
+        @pl.when(at < slices - 1)
+        def _():
+            final_copy(k, at, part, fin_send.at[k, 0], right).wait_send()
+
+        @pl.when(at > 0)
+        def _():
+            final_copy(k, at, part, fin_send.at[k, 1], left).wait_send()
+
+        local_copy(k).wait()
+
+    def chain(k, stage):
+        if not 0 <= k < CHUNKS:
+            return
+        if stage == "first":
+            sums(k, slices - 1)
+        elif stage == "middle":
+            for d in range(slices - 2, 1, -1):
+                sums(k, d)
+        elif stage == "last":
+            if slices > 2:
+                sums(k, 1)
+        elif stage == "finish":
+            finish(k)
+        elif stage == "near":
+            passes(k, 1)
+        elif stage == "far":
+            for d in range(2, slices - 1):
+                passes(k, d)
+        elif stage == "farthest":
+            if slices > 2:
+                passes(k, slices - 1)
 
     last = len(items) - 1
     for item in range(len(items)):
+        k = item - exp_local
         forward(item)
         if item < last:
             start_own(item + 1)
@@ -250,27 +423,42 @@
                 from_core(item, [source])
                 hidden_units(source, item)
         else:
+            chain(k - 1, "middle")
+            chain(k - 2, "far")
             second(item)
+            chain(k - 1, "last")
+            chain(k - 2, "farthest")
             third(item)
             from_core(item, [sibling, sib_x] + sib_y + sib_corners)
-            outputs(item - exp_local)
+            chain(k - 1, "finish")
+            outputs(k)
+            chain(k, "first")
+            chain(k - 1, "near")
+    end = CHUNKS - 1
+    chain(end, "middle")
+    chain(end - 1, "far")
+    chain(end, "last")
+    chain(end - 1, "farthest")
+    for stage in ("finish", "near", "far", "farthest"):
+        chain(end, stage)
     for copy in sent:
         copy.wait_send()
-    for copy in outs:
-        copy.wait()
+    for k in range(CHUNKS):
+        drain(k)
 
 
 def shards(flow_state, norm_gain, expert_ids, gate_weights, w_gate, w_up, w_down):
     rows, width = flow_state.shape
     exp_local, hidden, _ = w_gate.shape
     groups = lax.axis_size("expert")
+    slices = lax.axis_size("tensor")
     experts = exp_local * groups
     n_pieces = exp_local * (4 + CHUNKS)
     weights = pltpu.VMEM((experts, hidden, width), jnp.bfloat16)
     any_space = pl.BlockSpec(memory_space=pl.ANY)
     vmem = pl.BlockSpec(memory_space=pltpu.VMEM)
-    partial = pl.pallas_call(
-        functools.partial(kernel, groups),
+    return pl.pallas_call(
+        functools.partial(kernel, groups, slices),
         out_shape=jax.ShapeDtypeStruct((rows, width), jnp.bfloat16),
         in_specs=[any_space, vmem, vmem, vmem, any_space, any_space, any_space],
         out_specs=any_space,
@@ -281,11 +469,18 @@
             pltpu.VMEM((rows, width), jnp.bfloat16),
             pltpu.VMEM((rows, width), jnp.bfloat16),
             pltpu.VMEM((experts, rows, hidden), jnp.bfloat16),
+            pltpu.VMEM((CHUNKS, slices + 1, rows // slices, width // CHUNKS), jnp.bfloat16),
+            pltpu.VMEM((rows // slices, width), jnp.bfloat16),
             pltpu.SemaphoreType.DMA((n_pieces, groups)),
             pltpu.SemaphoreType.DMA((groups // 4 + 1, n_pieces, groups)),
-            pltpu.SemaphoreType.DMA((3,)),
+            pltpu.SemaphoreType.DMA((4,)),
             pltpu.SemaphoreType.DMA,
             pltpu.SemaphoreType.DMA((CHUNKS,)),
+            pltpu.SemaphoreType.DMA((CHUNKS, slices + 1)),
+            pltpu.SemaphoreType.DMA((CHUNKS, slices)),
+            pltpu.SemaphoreType.DMA((CHUNKS, 2)),
+            pltpu.SemaphoreType.DMA((CHUNKS, slices)),
+            pltpu.SemaphoreType.DMA((CHUNKS, slices)),
         ],
         compiler_params=pltpu.CompilerParams(
             collective_id=0, has_side_effects=True, vmem_limit_bytes=66 * 1000 * 1000
@@ -299,8 +494,6 @@
         w_up,
         w_down,
     )
-    summed = lax.psum(partial, "tensor").astype(jnp.float32)
-    return (flow_state.astype(jnp.float32) + summed).astype(jnp.bfloat16)
 
 
 def solution(mesh):

time: 341 us -> 257 us (0.75)
  waiting for transfers between devices: 155 us -> 0 us
  Pallas kernels: 160 us -> 248 us
  between operations: 13.4 us -> 0.01 us
  other arithmetic: 7.77 us -> 0 us
  local copies, waits for them, and re-layouts: 3.55 us -> 8.34 us
    psum x1 -> x0, waiting for transfers between devices: 155 us -> none  [shards(): summed = lax.psum(partial, 'tensor').astype(jnp.float32)]
    pallas_call x1, Pallas kernels: 160 us -> 248 us  [shards(): pl.pallas_call(functools.partial(kernel, groups, slices), out_shape=jax.S...]
    convert_element_type x1 -> x0, other arithmetic: 7.77 us -> none  [shards(): return (flow_state.astype(jnp.float32) + summed).astype(jnp.bfloat16)]
    unnamed x2 -> x3, local copies, waits for them, and re-layouts: 3.55 us -> 8.34 us
  transfers between devices with their start and end apart: 1 -> 0, of which waited for: 1 -> 0; matrix products, arithmetic and copies ran while one was open for 0% -> 0% of each run, Pallas kernels for 0% -> 0%
where the time goes in v2:
time: 257 us; the launch traced here: 256 us
  Pallas kernels  248 us (96%)
  local copies, waits for them, and re-layouts  8.34 us (3%)
    pallas_call x1, Pallas kernels, shards(): pl.pallas_call(functools.partial(kernel, groups, slices), out_shape=jax.S...  248 us
    unnamed x3, local copies, waits for them, and re-layouts  8.34 us

profile of v2, /device:TPU:0, one launch (start us, length us, event | category | flops | bytes accessed | tf_op | source)
XLA Modules:
  0.0 256.3 jit_solution(14061395561111068162)
XLA Ops:
  0.0 1.8 copy.8.ids_ref
  1.8 1.8 copy.9.gw_ref
  3.6 247.9 %shard_map.73 = bf16[1024,2048]{1,0:T(8,128)(2,1)} custom-call(bf16[1024,2048]{1,0:T(8,128)(2,1)} %state_hbm.1, f32[1,2048]{1,0:T(1,128)} %bitcast.1, s32[1024,6]{1,0:T(8,128)} %copy.8.ids_ref, f32[1024,6]{1,0:T(8,128)} %copy.9.gw_ref, bf16[2,176,2048]{2,1,0:T(8,128)(2,1)} %wg_hbm.1, bf16[2,176,2048]{2,1,0:T(8,128)(2,1)} %wu_hbm.1, bf16[2,176,2048]{2,1,0:T(8,128)(2,1)} %wd_hbm.1), custom_call_target="tpu_custom_call" | custom-call | tf_op jit(solution)/shard_map/pallas_call | solution.py:460
  251.5 4.8 %copy.11 = bf16[1024,2048]{1,0:T(8,128)(2,1)} copy(bf16[1024,2048]{1,0:T(8,128)(2,1)} %shard_map.73) | data formatting | bytes 8388608

commit v3 on v2

--- a/solution.py
+++ b/solution.py
@@ -8,7 +8,7 @@
 from jax.sharding import PartitionSpec as P
 
 MESH = pl.DeviceIdType.MESH
-CHUNKS = 4
+CHUNKS = 8
 ROW_TILE = 256
 
 
@@ -423,24 +423,24 @@
                 from_core(item, [source])
                 hidden_units(source, item)
         else:
+            chain(k - 6, "farthest")
+            chain(k - 5, "far")
+            second(item)
+            chain(k - 4, "near")
+            chain(k - 3, "finish")
+            third(item)
+            chain(k - 2, "last")
             chain(k - 1, "middle")
-            chain(k - 2, "far")
-            second(item)
-            chain(k - 1, "last")
-            chain(k - 2, "farthest")
-            third(item)
             from_core(item, [sibling, sib_x] + sib_y + sib_corners)
-            chain(k - 1, "finish")
             outputs(k)
             chain(k, "first")
-            chain(k - 1, "near")
-    end = CHUNKS - 1
-    chain(end, "middle")
-    chain(end - 1, "far")
-    chain(end, "last")
-    chain(end - 1, "farthest")
-    for stage in ("finish", "near", "far", "farthest"):
-        chain(end, stage)
+    for k in range(CHUNKS, CHUNKS + 6):
+        chain(k - 6, "farthest")
+        chain(k - 5, "far")
+        chain(k - 4, "near")
+        chain(k - 3, "finish")
+        chain(k - 2, "last")
+        chain(k - 1, "middle")
     for copy in sent:
         copy.wait_send()
     for k in range(CHUNKS):

time: 257 us -> 244 us (0.949)
  Pallas kernels: 248 us -> 235 us
    pallas_call x1, Pallas kernels: 248 us -> 235 us  [shards(): pl.pallas_call(functools.partial(kernel, groups, slices), out_shape=jax.S...]
where the time goes in v3:
time: 244 us
  Pallas kernels  235 us (96%)
  local copies, waits for them, and re-layouts  8.34 us (3%)
    pallas_call x1, Pallas kernels, shards(): pl.pallas_call(functools.partial(kernel, groups, slices), out_shape=jax.S...  235 us
    unnamed x3, local copies, waits for them, and re-layouts  8.34 us

profile of v3, /device:TPU:0, one launch (start us, length us, event | category | flops | bytes accessed | tf_op | source)
XLA Modules:
  0.0 243.8 jit_solution(2182627857476678982)
XLA Ops:
  0.0 1.8 copy.8.ids_ref
  1.8 1.8 copy.9.gw_ref
  3.6 235.5 %shard_map.73 = bf16[1024,2048]{1,0:T(8,128)(2,1)} custom-call(bf16[1024,2048]{1,0:T(8,128)(2,1)} %state_hbm.1, f32[1,2048]{1,0:T(1,128)} %bitcast.1, s32[1024,6]{1,0:T(8,128)} %copy.8.ids_ref, f32[1024,6]{1,0:T(8,128)} %copy.9.gw_ref, bf16[2,176,2048]{2,1,0:T(8,128)(2,1)} %wg_hbm.1, bf16[2,176,2048]{2,1,0:T(8,128)(2,1)} %wu_hbm.1, bf16[2,176,2048]{2,1,0:T(8,128)(2,1)} %wd_hbm.1), custom_call_target="tpu_custom_call" | custom-call | tf_op jit(solution)/shard_map/pallas_call | solution.py:460
  239.0 4.8 %copy.11 = bf16[1024,2048]{1,0:T(8,128)(2,1)} copy(bf16[1024,2048]{1,0:T(8,128)(2,1)} %shard_map.73) | data formatting | bytes 8388608
